TPU v7x, 32 devices: a whole 2x2x4 slice. The times are simulated.
32 devices in a mesh: dp: 8 (over y, x, core), vocab: 4 (over z).
Axes of the slice: x: 2, y: 2, z: 4, core: 2. Of those that a mesh axis runs over, the one named last changes fastest.
Arguments:
- hidden: bfloat16 [128, 5120], P('dp', 'vocab')
- inputs: bfloat16 [128, 3072], P('dp', 'vocab'), may hold values from -6 to 6
- gain: float32 [5120], replicated, may hold values from 0.5 to 1.5
- unembed: bfloat16 [6400, 5120], P(('dp', 'vocab'))
- proj_out: bfloat16 [5120, 128], replicated, may hold values from -6 to 6
- proj_in: bfloat16 [3072, 128], replicated, may hold values from -0.109375 to 0.109375
- targets: int32 [128], replicated, may hold values from 0 to 6399
- segment_ids: int32 [128], replicated, may hold values from 0 to 3, never falling along the last dimension, each value on 1 to 96 neighbouring positions
- store: bfloat16 [2048, 16384], P(('dp', 'vocab')), may hold values from -0.005859375 to 0.005859375
Outputs:
- scores: float32 [4, 2048], P(None, ('dp', 'vocab'))
- logprob: float32 [128], P('dp')
Inputs may be any that keep to these rules, and one draw needn't show every extreme that they name: `segment_ids`: each sequence is a run of consecutive tokens; ids never fall; each sequence has 1 to 96 tokens and one has exactly 96.
All inputs are finite; a program needn't handle non-finite values.
Results may differ from a plain program's by a relative error of at most 0.0074.
Values may be sent and summed in bfloat16 or wider, within the bound.
No kernel may reach another device: no remote copies, remote signals or barrier semaphores. Data moves between devices by JAX's collectives and lax.ppermute only.
A program may use at most 64 MiB of HBM per device.

v0:
```python
import jax
import jax.numpy as jnp
from jax import lax
from jax.sharding import PartitionSpec as P

D = 5120
V_DEV = 200
PROJ = 128
EPSILON = 1e-06


def body(hidden, inputs, gain, unembed, proj_out, proj_in, targets, segment_ids, store):
    token_count = targets.shape[0]
    seq_count = token_count // 32
    local_rows = hidden.shape[0]
    token_part = lax.all_gather(hidden, "vocab", axis=1, tiled=True)
    gathered = lax.all_gather(token_part, "dp", axis=0, tiled=True)
    hidden_f32 = gathered.astype(jnp.float32)
    root_mean = jnp.sqrt(jnp.mean(hidden_f32 * hidden_f32, axis=1) + EPSILON)
    normed = (hidden_f32 * gain[None, :] / root_mean[:, None]).astype(jnp.bfloat16)
    logits = lax.dot_general(
        normed, unembed, (((1,), (1,)), ((), ())), preferred_element_type=jnp.float32
    )
    device_pos = lax.axis_index("dp") * lax.axis_size("vocab") + lax.axis_index("vocab")
    column_ids = device_pos * V_DEV + jnp.arange(V_DEV, dtype=jnp.int32)
    onehot = targets[:, None] == column_ids[None, :]
    local_peak = jnp.max(logits, axis=1)
    local_target = jnp.sum(jnp.where(onehot, logits, jnp.zeros_like(logits)), axis=1)
    row_peak = lax.pmax(local_peak, ("dp", "vocab"))
    shifted = jnp.exp(logits - row_peak[:, None])
    row_total, target_logit = lax.psum((jnp.sum(shifted, axis=1), local_target), ("dp", "vocab"))
    logprob = target_logit - row_peak - jnp.log(row_total)
    logprob_rows = lax.dynamic_slice_in_dim(logprob, lax.axis_index("dp") * local_rows, local_rows)
    dlogits = (onehot.astype(jnp.float32) - shifted / row_total[:, None]).astype(jnp.bfloat16)
    dnormed = jnp.dot(dlogits, unembed, preferred_element_type=jnp.float32)
    weighted = dnormed * gain[None, :]
    part_proj = jnp.dot(weighted, proj_out.astype(jnp.float32), precision=lax.Precision.HIGHEST)
    part_dot = jnp.sum(weighted * hidden_f32, axis=1)
    grad_proj, grad_dot = lax.psum((part_proj, part_dot), ("dp", "vocab"))
    hidden_proj = jnp.dot(gathered, proj_out, preferred_element_type=jnp.float32)
    out_grad = (
        grad_proj / root_mean[:, None] - hidden_proj * (grad_dot / (D * root_mean**3))[:, None]
    )
    slice_width = inputs.shape[1]
    proj_slice = lax.dynamic_slice_in_dim(
        proj_in, lax.axis_index("vocab") * slice_width, slice_width, 0
    )
    local_proj = jnp.dot(inputs, proj_slice, preferred_element_type=jnp.float32)
    summed_proj = lax.psum(local_proj, "vocab")
    in_proj = lax.all_gather(summed_proj, "dp", axis=0, tiled=True)
    member = (segment_ids[:, None] == jnp.arange(seq_count, dtype=jnp.int32)[None, :]).astype(
        jnp.float32
    )
    spread = (member[:, :, None] * out_grad[:, None, :]).reshape(token_count, seq_count * PROJ)
    seq_grads = lax.dot_general(
        spread, in_proj, (((0,), (0,)), ((), ())), precision=lax.Precision.HIGHEST
    )
    seq_grads = seq_grads.reshape(seq_count, PROJ * PROJ).astype(jnp.bfloat16)
    scores = lax.dot_general(
        seq_grads, store, (((1,), (1,)), ((), ())), preferred_element_type=jnp.float32
    )
    return (scores, logprob_rows)


def solution(mesh):
    in_specs = (
        P("dp", "vocab"),
        P("dp", "vocab"),
        P(),
        P(("dp", "vocab"), None),
        P(),
        P(),
        P(),
        P(),
        P(("dp", "vocab"), None),
    )
    out_specs = (P(None, ("dp", "vocab")), P("dp"))
    return jax.shard_map(body, mesh=mesh, in_specs=in_specs, out_specs=out_specs, check_vma=False)
```

profile of v0, /device:TPU:1, one launch (start us, length us, event | category | flops | bytes accessed | tf_op | source)
XLA Modules:
  0.0 315.6 jit_solution(14063403829248417648)
XLA Ops:
  7.2 0.0 all-gather.2.cloned.1.call-start
  7.2 13.9 %all_gather.9 = bf16[16,5120]{1,0:T(8,128)(2,1)} all-gather(bf16[16,1280]{1,0:T(8,128)(2,1)} %param.9), channel_id=1, replica_groups=mesh['dp'=8,'vocab'=4] {'vocab'}, dimensions={1}, use_global_device_ids=true | all-gather | bytes 204800 | tf_op jit(solution)/shard_map/all_gather | solution.py:16
  21.2 0.0 all-reduce.3.cloned.1.call-start
  21.3 1.1 convolution_bitcast_fusion
  22.3 8.7 %psum.38 = f32[16,128]{1,0:T(8,128)S(1)} all-reduce(f32[16,128]{1,0:T(8,128)S(1)} %convolution_bitcast_fusion), channel_id=1, replica_groups=mesh['dp'=8,'vocab'=4] {'vocab'}, use_global_device_ids=true, to_apply=%region_8.9 | all-reduce | flops 2048 | bytes 16384 | tf_op jit(solution)/shard_map/psum | solution.py:49
  31.0 15.7 %all_gather.11 = f32[128,128]{1,0:T(8,128)} all-gather(f32[16,128]{1,0:T(8,128)S(1)} %psum.38), channel_id=1, replica_groups=mesh['dp'=8,'vocab'=4] {'dp'}, dimensions={0}, use_global_device_ids=true | all-gather | bytes 73728 | tf_op jit(solution)/shard_map/all_gather | solution.py:50
  46.8 1.4 fusion.14
  48.1 1.0 all-gather.2.cloned.1.call-done
  49.1 1.6 fusion.2
  50.8 2.9 fusion.23
  53.7 38.0 %pmax.7 = f32[128]{0:T(128)S(1)} all-reduce(f32[128]{0:T(128)S(1)} %get-tuple-element.6), channel_id=1, replica_groups=mesh['dp'=8,'vocab'=4] {'dp','vocab'}, use_global_device_ids=true, to_apply=%region_2.3 | all-reduce | flops 128 | bytes 1024 | tf_op jit(solution)/shard_map/pmax | solution.py:29
  91.7 0.6 fusion.12
  92.3 41.1 %psum.35 = f32[128]{0:T(128)S(1)} all-reduce(f32[128]{0:T(128)} %get-tuple-element.3), channel_id=1, replica_groups=mesh['dp'=8,'vocab'=4] {'dp','vocab'}, use_global_device_ids=true, to_apply=%region_4.5 | all-reduce | flops 128 | bytes 1024 | tf_op jit(solution)/shard_map/psum | solution.py:31
  133.5 4.3 %fusion.3 = (f32[128]{0:T(128)}, f32[128,5120]{1,0:T(8,128)}) fusion(bf16[128,5120]{1,0:T(8,128)(2,1)S(1)} %copy-done.1, f32[5120]{0:T(1024)S(1)} %copy-done.4, bf16[200,5120]{1,0:T(8,128)(2,1)} %param.12, f32[128,200]{0,1:T(8,128)S(1)} %get-tuple-element.7, f32[128]{0:T(128)S(1)} %psum.35, f32[128]{0:T(128)S(1)} %pmax.7, s32[128]{0:T(128)S(1)} %copy-done.5, ...), kind=kOutput, calls=%fused_computation.7 | convolution fusion | flops 264918912 | bytes 6105888 | tf_op jit(solution)/shard_map/dot_general | solution.py:35
  137.8 39.5 %all-reduce = (f32[128]{0:T(128)}, f32[128]{0:T(128)S(1)}) all-reduce(f32[128]{0:T(128)} %get-tuple-element.8, f32[128]{0:T(128)} %get-tuple-element.2), channel_id=1, replica_groups=mesh['dp'=8,'vocab'=4] {'dp','vocab'}, use_global_device_ids=true, to_apply=%region_7.8 | all-reduce | flops 256 | bytes 2048 | tf_op jit(solution)/shard_map/psum | solution.py:39
  177.2 0.5 log_subtract_fusion
  177.7 4.1 %fusion.24 = f32[128,128]{1,0:T(8,128)} fusion(f32[128,5120]{1,0:T(8,128)} %get-tuple-element.9, bf16[5120,128]{1,0:T(8,128)(2,1)} %param.13), kind=kOutput, calls=%fused_computation.38 | convolution fusion | flops 1006632960 | bytes 3997696 | tf_op jit(solution)/shard_map/dot_general | solution.py:37
  181.9 0.7 fusion.21
  182.6 0.6 dynamic_slice.7
  183.2 121.7 %all-reduce.3.cloned.1.call-done = f32[128,128]{1,0:T(8,128)} async-done(((f32[128,128]{1,0:T(8,128)}), f32[128,128]{1,0:T(8,128)}) %all-reduce.3.cloned.1.call-update) | async-done | bytes 65552 | tf_op jit(solution)/shard_map/psum | solution.py:39
  304.9 1.8 fusion.6
  306.7 0.2 broadcast_multiply_fusion
  306.9 0.6 convolution_convert_fusion
  307.6 1.2 fusion.25
  (19 shorter events, 0.1 us)
Async XLA Ops:
  7.2 300.4 %copy-start = (bf16[64,16384]{1,0:T(8,128)(2,1)S(1)}, bf16[64,16384]{1,0:T(8,128)(2,1)}, u32[]{:S(2)}) copy-start(bf16[64,16384]{1,0:T(8,128)(2,1)} %param.17) | copy-start | bytes 6291460
  7.2 43.6 %copy-start.4 = (f32[5120]{0:T(1024)S(1)}, f32[5120]{0:T(1024)}, u32[]{:S(2)}) copy-start(f32[5120]{0:T(1024)} %param.11) | copy-start | bytes 61444
  7.2 41.9 %all-gather.2.cloned.1.call-start = ((), (), s32[]{:S(2)}) async-start(), calls=%async_computation | async-start | bytes 1474560 | tf_op jit(solution)/shard_map/all_gather | solution.py:17
  21.2 283.7 %all-reduce.3.cloned.1.call-start = ((), (), s32[]{:S(2)}) async-start(), calls=%async_computation.1 | async-start | bytes 131072 | tf_op jit(solution)/shard_map/psum | solution.py:39
  50.8 40.9 %copy-start.5 = (s32[128]{0:T(128)S(1)}, s32[128]{0:T(128)}, u32[]{:S(2)}) copy-start(s32[128]{0:T(128)} %param.15) | copy-start | bytes 1540
  50.8 82.7 %copy-start.1 = (bf16[128,5120]{1,0:T(8,128)(2,1)S(1)}, bf16[128,5120]{1,0:T(8,128)(2,1)}, u32[]{:S(2)}) copy-start(bf16[128,5120]{1,0:T(8,128)(2,1)} %all-gather.2.cloned.1.call-done) | copy-start | bytes 3932164
  177.7 4.8 %copy-start.6 = (f32[128]{0:T(128)S(1)}, f32[128]{0:T(128)}, u32[]{:S(2)}) copy-start(f32[128]{0:T(128)} %log_subtract_fusion) | copy-start | bytes 1540
  181.8 124.8 %copy-start.3 = (f32[128,4]{1,0:T(8,128)S(1)}, f32[128,4]{1,0:T(8,128)}, u32[]{:S(2)}) copy-start(f32[128,4]{1,0:T(8,128)} %fusion.14) | copy-start | bytes 6148
  181.8 125.0 %copy-start.2 = (f32[128,128]{1,0:T(8,128)S(1)}, f32[128,128]{1,0:T(8,128)}, u32[]{:S(2)}) copy-start(f32[128,128]{1,0:T(8,128)} %all_gather.11) | copy-start | bytes 196612
Sparse Core Ops, SparseCore 0:
  21.3 27.7 all-gather.1
  182.0 122.8 all-reduce.2
where the time goes:
time: 316 us
  blocking collectives  157 us (50%)
  waiting for transfers between devices  123 us (39%)
  matrix products  16 us (5%)
  between operations  14.2 us (4%)
  other arithmetic  5.06 us (2%)
    psum x1, waiting for transfers between devices, body(): grad_proj, grad_dot = lax.psum((part_proj, part_dot), ('dp', 'vocab'))  122 us
    psum x1, blocking collectives, body(): lax.psum((jnp.sum(shifted, axis=1), local_target), ('dp', 'vocab'))  41.1 us
    psum x1, blocking collectives, body(): grad_proj, grad_dot = lax.psum((part_proj, part_dot), ('dp', 'vocab'))  39.5 us
    pmax x1, blocking collectives, body(): row_peak = lax.pmax(local_peak, ('dp', 'vocab'))  38 us
    all_gather x1, blocking collectives, body(): in_proj = lax.all_gather(summed_proj, 'dp', axis=0, tiled=True)  15.7 us
    all_gather x1, blocking collectives, body(): token_part = lax.all_gather(hidden, 'vocab', axis=1, tiled=True)  13.9 us
    psum x1, blocking collectives, body(): summed_proj = lax.psum(local_proj, 'vocab')  8.68 us
  transfers between devices with their start and end apart: 2, of which 2 were waited for; matrix products, arithmetic and copies ran while one was open for 1% of the time, Pallas kernels for 0%

commit v1 on v0

--- a/solution.py
+++ b/solution.py
@@ -28,7 +28,9 @@
     local_target = jnp.sum(jnp.where(onehot, logits, jnp.zeros_like(logits)), axis=1)
     row_peak = lax.pmax(local_peak, ("dp", "vocab"))
     shifted = jnp.exp(logits - row_peak[:, None])
-    row_total, target_logit = lax.psum((jnp.sum(shifted, axis=1), local_target), ("dp", "vocab"))
+    row_total, target_logit = lax.psum(
+        lax.psum((jnp.sum(shifted, axis=1), local_target), "vocab"), "dp"
+    )
     logprob = target_logit - row_peak - jnp.log(row_total)
     logprob_rows = lax.dynamic_slice_in_dim(logprob, lax.axis_index("dp") * local_rows, local_rows)
     dlogits = (onehot.astype(jnp.float32) - shifted / row_total[:, None]).astype(jnp.bfloat16)

time: 316 us -> 297 us (0.940)
  blocking collectives: 157 us -> 125 us
  waiting for transfers between devices: 123 us -> 137 us
    psum x1, blocking collectives: 41.1 us -> 15.9 us  [body(): lax.psum(lax.psum((jnp.sum(shifted, axis=1), local_target), 'vocab'), 'dp')]
    all_gather x1, waiting for transfers between devices: 0.98 us -> 25.3 us  [body(): gathered = lax.all_gather(token_part, 'dp', axis=0, tiled=True)]
    psum x1, waiting for transfers between devices: 122 us -> 112 us  [body(): grad_proj, grad_dot = lax.psum((part_proj, part_dot), ('dp', 'vocab'))]
    all_gather x1, blocking collectives: 15.7 us -> 11.3 us  [body(): in_proj = lax.all_gather(summed_proj, 'dp', axis=0, tiled=True)]
    psum x1, blocking collectives: 39.5 us -> 36.2 us  [body(): grad_proj, grad_dot = lax.psum((part_proj, part_dot), ('dp', 'vocab'))]
where the time goes in v1:
time: 297 us
  waiting for transfers between devices  137 us (46%)
  blocking collectives  125 us (42%)
  matrix products  16 us (5%)
  between operations  14.2 us (5%)
  other arithmetic  3.87 us (1%)
    psum x1, waiting for transfers between devices, body(): grad_proj, grad_dot = lax.psum((part_proj, part_dot), ('dp', 'vocab'))  112 us
    pmax x1, blocking collectives, body(): row_peak = lax.pmax(local_peak, ('dp', 'vocab'))  38.3 us
    psum x1, blocking collectives, body(): grad_proj, grad_dot = lax.psum((part_proj, part_dot), ('dp', 'vocab'))  36.2 us
    all_gather x1, waiting for transfers between devices, body(): gathered = lax.all_gather(token_part, 'dp', axis=0, tiled=True)  25.3 us
    psum x1, blocking collectives, body(): lax.psum(lax.psum((jnp.sum(shifted, axis=1), local_target), 'vocab'), 'dp')  15.9 us
    all_gather x1, blocking collectives, body(): token_part = lax.all_gather(hidden, 'vocab', axis=1, tiled=True)  13.9 us
    all_gather x1, blocking collectives, body(): in_proj = lax.all_gather(summed_proj, 'dp', axis=0, tiled=True)  11.3 us
    psum x1, blocking collectives, body(): summed_proj = lax.psum(local_proj, 'vocab')  9.52 us
  transfers between devices with their start and end apart: 2, of which 2 were waited for; matrix products, arithmetic and copies ran while one was open for 1% of the time, Pallas kernels for 0%

profile of v1, /device:TPU:1, one launch (start us, length us, event | category | flops | bytes accessed | tf_op | source)
XLA Modules:
  0.0 297.0 jit_solution(1838450184745530539)
XLA Ops:
  7.2 0.0 all-gather.2.cloned.1.call-start
  7.2 13.9 %all_gather.9 = bf16[16,5120]{1,0:T(8,128)(2,1)} all-gather(bf16[16,1280]{1,0:T(8,128)(2,1)} %param.9), channel_id=1, replica_groups=mesh['dp'=8,'vocab'=4] {'vocab'}, dimensions={1}, use_global_device_ids=true | all-gather | bytes 204800 | tf_op jit(solution)/shard_map/all_gather | solution.py:16
  21.2 0.0 all-gather.2.cloned.1.call-update
  21.2 0.0 all-reduce.4.cloned.1.call-start
  21.2 1.1 convolution_bitcast_fusion
  22.3 1.4 fusion.14
  23.7 25.3 %all-gather.2.cloned.1.call-done = bf16[128,5120]{1,0:T(8,128)(2,1)} async-done(((bf16[16,5120]{1,0:T(8,128)(2,1)}), bf16[128,5120]{1,0:T(8,128)(2,1)}) %all-gather.2.cloned.1.call-update) | async-done | bytes 1310736 | tf_op jit(solution)/shard_map/all_gather | solution.py:17
  49.0 1.6 fusion.2
  50.7 3.4 %fusion.23 = (f32[128]{0:T(128)}, f32[128,200]{0,1:T(8,128)S(1)}) fusion(bf16[200,5120]{1,0:T(8,128)(2,1)} %param.12, bf16[128,5120]{1,0:T(8,128)(2,1)} %all-gather.2.cloned.1.call-done, f32[128]{0:T(128)S(1)} %add_sqrt_fusion, f32[5120]{0:T(1024)} %param.11), kind=kOutput, calls=%fused_computation.37 | convolution fusion | flops 264790912 | bytes 3482624 | tf_op jit(solution)/shard_map/dot_general | solution.py:21
  54.1 38.3 %pmax.7 = f32[128]{0:T(128)S(1)} all-reduce(f32[128]{0:T(128)} %get-tuple-element.9), channel_id=1, replica_groups=mesh['dp'=8,'vocab'=4] {'dp','vocab'}, use_global_device_ids=true, to_apply=%region_2.3 | all-reduce | flops 128 | bytes 1024 | tf_op jit(solution)/shard_map/pmax | solution.py:29
  92.4 0.6 fusion.12
  93.0 9.5 %all-reduce.1 = (f32[16,128]{1,0:T(8,128)S(1)}, f32[128]{0:T(128)}, f32[128]{0:T(128)}) all-reduce(f32[16,128]{1,0:T(8,128)S(1)} %convolution_bitcast_fusion, f32[128]{0:T(128)} %get-tuple-element.3, f32[128]{0:T(128)} %get-tuple-element.2), channel_id=1, replica_groups=mesh['dp'=8,'vocab'=4] {'vocab'}, use_global_device_ids=true, to_apply=%region_9.10 | all-reduce | flops 2304 | bytes 18432 | tf_op jit(solution)/shard_map/psum | solution.py:51
  102.6 15.9 %all-reduce = (f32[128]{0:T(128)S(1)}, f32[128]{0:T(128)}) all-reduce(f32[128]{0:T(128)} %get-tuple-element.7, f32[128]{0:T(128)} %get-tuple-element.8), channel_id=1, replica_groups=mesh['dp'=8,'vocab'=4] {'dp'}, use_global_device_ids=true, to_apply=%region_5.6 | all-reduce | flops 256 | bytes 2048 | tf_op jit(solution)/shard_map/psum | solution.py:31
  118.5 3.8 %fusion.3 = (f32[128]{0:T(128)S(1)}, f32[128,5120]{1,0:T(8,128)}) fusion(bf16[128,5120]{1,0:T(8,128)(2,1)S(1)} %copy-done.1, f32[5120]{0:T(1024)S(1)} %copy-done.3, bf16[200,5120]{1,0:T(8,128)(2,1)} %param.12, f32[128,200]{0,1:T(8,128)S(1)} %get-tuple-element.10, f32[128]{0:T(128)S(1)} %get-tuple-element.4, f32[128]{0:T(128)S(1)} %pmax.7, s32[128]{0:T(128)} %param.15, ...), kind=kOutput, calls=%fused_computation.7 | convolution fusion | flops 264918912 | bytes 6105888 | tf_op jit(solution)/shard_map/dot_general | solution.py:37
  122.3 36.2 %psum.52 = f32[128]{0:T(128)S(1)} all-reduce(f32[128]{0:T(128)S(1)} %get-tuple-element.11), channel_id=1, replica_groups=mesh['dp'=8,'vocab'=4] {'dp','vocab'}, use_global_device_ids=true, to_apply=%region_8.9 | all-reduce | flops 128 | bytes 1024 | tf_op jit(solution)/shard_map/psum | solution.py:41
  158.5 4.1 %fusion.24 = f32[128,128]{1,0:T(8,128)} fusion(f32[128,5120]{1,0:T(8,128)} %get-tuple-element.12, bf16[5120,128]{1,0:T(8,128)(2,1)} %param.13), kind=kOutput, calls=%fused_computation.38 | convolution fusion | flops 1006632960 | bytes 3997696 | tf_op jit(solution)/shard_map/dot_general | solution.py:39
  162.6 0.0 all-reduce.4.cloned.1.call-update
  162.7 0.6 dynamic_slice.7
  163.3 11.3 %all_gather.11 = f32[128,128]{1,0:T(8,128)S(1)} all-gather(f32[16,128]{1,0:T(8,128)S(1)} %get-tuple-element.6), channel_id=1, replica_groups=mesh['dp'=8,'vocab'=4] {'dp'}, dimensions={0}, use_global_device_ids=true | all-gather | bytes 73728 | tf_op jit(solution)/shard_map/all_gather | solution.py:52
  174.6 111.6 %all-reduce.4.cloned.1.call-done = f32[128,128]{1,0:T(8,128)} async-done(((f32[128,128]{1,0:T(8,128)}), f32[128,128]{1,0:T(8,128)}) %all-reduce.4.cloned.1.call-update) | async-done | bytes 65552 | tf_op jit(solution)/shard_map/psum | solution.py:41
  286.2 1.8 fusion.6
  288.0 0.2 broadcast_multiply_fusion
  288.2 0.6 convolution_convert_fusion
  288.9 1.2 fusion.25
  (29 shorter events, 0.1 us)
Async XLA Ops:
  7.2 281.7 %copy-start = (bf16[64,16384]{1,0:T(8,128)(2,1)S(1)}, bf16[64,16384]{1,0:T(8,128)(2,1)}, u32[]{:S(2)}) copy-start(bf16[64,16384]{1,0:T(8,128)(2,1)} %param.17) | copy-start | bytes 6291460
  7.2 41.8 %all-gather.2.cloned.1.call-start = ((), (), s32[]{:S(2)}) async-start(), calls=%async_computation | async-start | bytes 1474560 | tf_op jit(solution)/shard_map/all_gather | solution.py:17
  21.2 265.0 %all-reduce.4.cloned.1.call-start = ((), (), s32[]{:S(2)}) async-start(), calls=%async_computation.1 | async-start | bytes 131072 | tf_op jit(solution)/shard_map/psum | solution.py:41
  50.7 3.5 %copy-start.9 = (f32[128]{0:T(128)}, f32[128]{0:T(128)S(1)}, u32[]{:S(2)}) copy-start(f32[128]{0:T(128)S(1)} %fusion.2) | copy-start | bytes 1540
  50.7 3.4 %copy-start.7 = (f32[128]{0:T(128)}, f32[128]{0:T(128)S(1)}, u32[]{:S(2)}) copy-start(f32[128]{0:T(128)S(1)} %add_sqrt_fusion) | copy-start | bytes 1540
  50.7 41.7 %copy-start.4 = (s32[128]{0:T(128)S(1)}, s32[128]{0:T(128)}, u32[]{:S(2)}) copy-start(s32[128]{0:T(128)} %param.15) | copy-start | bytes 1540
  50.7 67.8 %copy-start.1 = (bf16[128,5120]{1,0:T(8,128)(2,1)S(1)}, bf16[128,5120]{1,0:T(8,128)(2,1)}, u32[]{:S(2)}) copy-start(bf16[128,5120]{1,0:T(8,128)(2,1)} %all-gather.2.cloned.1.call-done) | copy-start | bytes 3932164
  50.7 67.8 %copy-start.3 = (f32[5120]{0:T(1024)S(1)}, f32[5120]{0:T(1024)}, u32[]{:S(2)}) copy-start(f32[5120]{0:T(1024)} %param.11) | copy-start | bytes 61444
  118.5 3.8 %copy-start.5 = (f32[128]{0:T(128)}, f32[128]{0:T(128)S(1)}, u32[]{:S(2)}) copy-start(f32[128]{0:T(128)S(1)} %get-tuple-element.4) | copy-start | bytes 1540
  122.3 40.3 %copy-start.11 = (f32[128]{0:T(128)S(1)}, f32[128]{0:T(128)}, u32[]{:S(2)}) copy-start(f32[128]{0:T(128)} %get-tuple-element.5) | copy-start | bytes 1540
  122.3 40.3 %copy-start.10 = (f32[128]{0:T(128)S(1)}, f32[128]{0:T(128)}, u32[]{:S(2)}) copy-start(f32[128]{0:T(128)} %copy-done.9) | copy-start | bytes 1540
  122.3 40.3 %copy-start.6 = (f32[128]{0:T(128)S(1)}, f32[128]{0:T(128)}, u32[]{:S(2)}) copy-start(f32[128]{0:T(128)} %copy-done.5) | copy-start | bytes 1540
  158.5 127.7 %copy-start.8 = (f32[128]{0:T(128)S(1)}, f32[128]{0:T(128)}, u32[]{:S(2)}) copy-start(f32[128]{0:T(128)} %copy-done.7) | copy-start | bytes 1540
  162.6 125.4 %copy-start.2 = (f32[128,4]{1,0:T(8,128)S(1)}, f32[128,4]{1,0:T(8,128)}, u32[]{:S(2)}) copy-start(f32[128,4]{1,0:T(8,128)} %fusion.14) | copy-start | bytes 6148
Sparse Core Ops, SparseCore 0:
  21.3 27.6 all-gather.1
  162.8 123.3 all-reduce.3
